TPU v7x, 32 devices: a whole 2x2x4 slice. The times are simulated.
32 devices in a mesh: blk: 16 (over z, y, core), rep: 2 (over x).
Axes of the slice: x: 2, y: 2, z: 4, core: 2. Of those that a mesh axis runs over, the one named last changes fastest.
Arguments:
- grad_out: bfloat16 [24576, 256], P('blk'), may hold values from -6 to 6
- pre_act: bfloat16 [24576, 256], P('blk'), may hold values from -6 to 6
- prev_pre: bfloat16 [24576, 256], P(('blk', 'rep')), may hold values from -6 to 6
- weight: bfloat16 [256, 256], replicated, may hold values from -0.375 to 0.375
- block_values: bfloat16 [3840, 128, 128], P(('blk', 'rep')), may hold values from -0.25 to 0.25
- block_rows: int32 [3840], P(('blk', 'rep')), may hold values from 0 to 11, as said below
- block_cols: int32 [3840], P(('blk', 'rep')), may hold values from 0 to 59
Outputs:
- grad_in: bfloat16 [24576, 256], P(('blk', 'rep'))
- grad_weight: float32 [256, 256], replicated
Inputs may be any that keep to these rules, and one draw needn't show every extreme that they name: The blocks of the 2 devices of one stripe sit at distinct (block_rows, block_cols) positions.
All inputs are finite; a program needn't handle non-finite values.
Results may differ from a plain program's by a relative error of at most 0.0049.
Values sent between devices are 32-bit elements; how exact they have to be, the bound alone decides.
A program may use at most 192 MiB of HBM per device.

v0:
```python
import math
import jax
import jax.numpy as jnp
from jax import lax
from jax.sharding import PartitionSpec as P

HALO = 2


def shifted(value, axis, by):
    devices = lax.axis_size(axis)
    return lax.ppermute(value, axis, [(i, (i + by) % devices) for i in range(devices)])


def local(grad_out, pre_act, prev_pre, weight, block_values, block_rows, block_cols):
    stripe_rows, width = grad_out.shape
    block_size = block_values.shape[1]
    stripe_blocks = stripe_rows // block_size
    spans = 2 * HALO + 1
    masked = grad_out * (pre_act > 0).astype(jnp.bfloat16)
    picked = masked.reshape(stripe_blocks, block_size, width)[block_rows]
    tiles = jnp.einsum("kab,kaf->kbf", block_values, picked, preferred_element_type=jnp.float32)
    window = jax.ops.segment_sum(tiles, block_cols, num_segments=spans * stripe_blocks)
    window = window.reshape(spans, stripe_rows, width)
    total = window[HALO]
    for position in range(spans):
        if position != HALO:
            total = total + shifted(window[position], "blk", position - HALO)
    mine = lax.psum_scatter(total, "rep", scatter_dimension=0, tiled=True)
    dy_rows = mine.astype(jnp.bfloat16)
    feats = jnp.maximum(prev_pre, jnp.zeros_like(prev_pre))
    weight_term = jnp.dot(feats.T, dy_rows, preferred_element_type=jnp.float32)
    node_count = stripe_rows * lax.axis_size("blk")
    grad_weight = lax.psum(weight_term, ("blk", "rep")) * (1.0 / math.sqrt(node_count))
    grad_in = (
        jnp.dot(dy_rows, weight.T, preferred_element_type=jnp.float32)
        * (prev_pre > 0).astype(jnp.float32)
    ).astype(jnp.bfloat16)
    return (grad_in, grad_weight)


def solution(mesh):
    in_specs = (
        P("blk", None),
        P("blk", None),
        P(("blk", "rep"), None),
        P(),
        P(("blk", "rep"), None, None),
        P(("blk", "rep")),
        P(("blk", "rep")),
    )
    out_specs = (P(("blk", "rep"), None), P())
    return jax.shard_map(local, mesh=mesh, in_specs=in_specs, out_specs=out_specs, check_vma=False)
```

profile of v0, /device:TPU:0, one launch (start us, length us, event | category | flops | bytes accessed | tf_op | source)
XLA Modules:
  0.0 365.0 jit_solution(13241581030041668142)
XLA Ops:
  7.2 0.0 copy-start
  7.2 0.0 reduce-scatter.2.cloned.1.call-start
  7.2 0.7 compare_select_fusion.1
  7.9 1.5 compare_select_fusion
  9.4 6.4 %gather_fusion = bf16[120,128,256]{2,1,0:T(8,128)(2,1)} fusion(bf16[12,128,256]{2,1,0:T(8,128)(2,1)S(1)} %bitcast.18, s32[1024]{0:T(1024)S(1)} %pad_clamp_fusion), kind=kCustom, calls=%fused_computation | custom fusion | bytes 15729120 | tf_op jit(solution)/shard_map/gather | solution.py:21
  15.8 12.1 %convolution_bitcast_fusion = f32[120,128,256]{1,2,0:T(8,128)} fusion(bf16[120,128,256]{2,1,0:T(8,128)(2,1)} %gather_fusion, bf16[120,128,128]{2,1,0:T(8,128)(2,1)} %param.11), kind=kOutput, calls=%fused_computation.2 | convolution fusion | flops 1006632960 | bytes 27525120 | tf_op jit(solution)/shard_map/kab,kaf->kbf/dot_general | solution.py:22
  27.9 15.6 %copy.11 = f32[120,128,256]{2,1,0:T(8,128)} copy(f32[120,128,256]{1,2,0:T(8,128)} %convolution_bitcast_fusion) | data formatting | bytes 31457280 | tf_op jit(solution)/shard_map/kab,kaf->kbf/dot_general | solution.py:22
  43.5 0.0 copy-start.3
  43.5 4.1 %broadcast_in_dim.9 = f32[60,128,256]{2,1,0:T(8,128)} broadcast(f32[]{:T(128)} %constant.2.clone.1), dimensions={} | broadcast | bytes 7864324 | tf_op jit(solution)/shard_map/broadcast_in_dim | solution.py:23
  47.5 0.0 copy-done.3
  47.5 38.0 %scatter_fusion = f32[60,128,256]{2,1,0:T(8,128)} fusion(f32[60,128,256]{2,1,0:T(8,128)} %broadcast_in_dim.9, s32[120]{0:T(128)S(1)} %copy-done.3, f32[120,128,256]{2,1,0:T(8,128)} %copy.11), kind=kCustom, calls=%fused_computation.1 | custom fusion | flops 3932160 | bytes 47186400 | tf_op jit(solution)/shard_map/scatter-add | solution.py:23
  85.6 3.9 %fusion.10 = (f32[12,128,256]{2,1,0:T(8,128)S(1)}, f32[12,128,256]{2,1,0:T(8,128)S(1)}, f32[12,128,256]{2,1,0:T(8,128)S(1)}, f32[12,128,256]{2,1,0:T(8,128)S(1)}, f32[12,128,256]{2,1,0:T(8,128)S(1)}) fusion(f32[60,128,256]{2,1,0:T(8,128)} %scatter_fusion), kind=kLoop, calls=%fused_computation.19 | loop fusion | bytes 15728640 | tf_op jit(solution)/shard_map/slice | solution.py:25
  89.4 3.0 collective-permute-start.3
  92.5 0.0 collective-permute-start.2
  92.5 4.4 %collective-permute-start.1 = (f32[1536,256]{1,0:T(8,128)S(1)}, f32[1536,256]{1,0:T(8,128)S(1)}, u32[]{:S(2)}, u32[]{:S(2)}) collective-permute-start(f32[1536,256]{1,0:T(8,128)S(1)} %bitcast.20), channel_id=1, source_target_pairs={{0,30},{2,0},{4,2},{6,4},{8,6},{10,8},{12,10},{14,12},{16,14},{18,... | collective-permute-start | bytes 4718600 | tf_op jit(solution)/shard_map/ppermute | solution.py:12
  96.9 0.3 collective-permute-start
  97.2 80.6 %collective-permute-done.3 = f32[1536,256]{1,0:T(8,128)S(1)} collective-permute-done((f32[1536,256]{1,0:T(8,128)S(1)}, f32[1536,256]{1,0:T(8,128)S(1)}, u32[]{:S(2)}, u32[]{:S(2)}) %collective-permute-start.3) | collective-permute-done | bytes 1572896 | tf_op jit(solution)/shard_map/ppermute | solution.py:12
  177.8 0.0 collective-permute-done.2
  177.8 0.0 collective-permute-done.1
  177.8 19.3 %collective-permute-done = f32[1536,256]{1,0:T(8,128)S(1)} collective-permute-done((f32[1536,256]{1,0:T(8,128)S(1)}, f32[1536,256]{1,0:T(8,128)S(1)}, u32[]{:S(2)}, u32[]{:S(2)}) %collective-permute-start) | collective-permute-done | bytes 1572896 | tf_op jit(solution)/shard_map/ppermute | solution.py:12
  197.1 1.7 fusion.2
  198.8 0.0 copy-start.2
  198.8 0.0 reduce-scatter.2.cloned.1.call-update
  198.8 0.0 all-reduce.2.cloned.1.call-start
  198.9 25.0 %reduce-scatter.2.cloned.1.call-done = f32[768,256]{1,0:T(8,128)} async-done(((f32[1536,256]{1,0:T(8,128)}), f32[768,256]{1,0:T(8,128)}) %reduce-scatter.2.cloned.1.call-update) | async-done | bytes 786448 | tf_op jit(solution)/shard_map/reduce_scatter | solution.py:29
  223.8 0.0 copy-done.2
  223.8 0.0 copy-start.1
  223.8 2.2 fusion.4
  226.0 0.0 all-reduce.2.cloned.1.call-update
  226.1 0.0 copy-done
  226.1 0.0 copy-done.1
  226.1 1.1 fusion.3
  227.1 129.4 %all-reduce.2.cloned.1.call-done = f32[256,256]{1,0:T(8,128)} async-done(((f32[256,256]{1,0:T(8,128)}), f32[256,256]{1,0:T(8,128)}) %all-reduce.2.cloned.1.call-update) | async-done | bytes 262160 | tf_op jit(solution)/shard_map/psum | solution.py:34
  356.5 1.7 broadcast_multiply_fusion
  (1 shorter events, 0.0 us)
Async XLA Ops:
  7.2 218.9 %copy-start = (bf16[256,256]{1,0:T(8,128)(2,1)S(1)}, bf16[256,256]{1,0:T(8,128)(2,1)}, u32[]{:S(2)}) copy-start(bf16[256,256]{1,0:T(8,128)(2,1)} %param.10) | copy-start | bytes 393220
  7.2 216.7 %reduce-scatter.2.cloned.1.call-start = ((), (), s32[]{:S(2)}) async-start(), calls=%async_computation.1 | async-start | bytes 2359296 | tf_op jit(solution)/shard_map/reduce_scatter | solution.py:29
  43.5 4.1 %copy-start.3 = (s32[120]{0:T(128)S(1)}, s32[120]{0:T(128)}, u32[]{:S(2)}) copy-start(s32[120]{0:T(128)} %param.13) | copy-start | bytes 1444
  89.4 88.4 %collective-permute-start.3 = (f32[1536,256]{1,0:T(8,128)S(1)}, f32[1536,256]{1,0:T(8,128)S(1)}, u32[]{:S(2)}, u32[]{:S(2)}) collective-permute-start(f32[1536,256]{1,0:T(8,128)S(1)} %bitcast.22), channel_id=1, source_target_pairs={{0,4},{2,6},{4,8},{6,10},{8,12},{10,14},{12,16},{14,18},{16,20},{1... | collective-permute-start | bytes 4718600 | tf_op jit(solution)/shard_map/ppermute | solution.py:12
  92.5 85.3 %collective-permute-start.2 = (f32[1536,256]{1,0:T(8,128)S(1)}, f32[1536,256]{1,0:T(8,128)S(1)}, u32[]{:S(2)}, u32[]{:S(2)}) collective-permute-start(f32[1536,256]{1,0:T(8,128)S(1)} %bitcast.21), channel_id=1, source_target_pairs={{0,2},{2,4},{4,6},{6,8},{8,10},{10,12},{12,14},{14,16},{16,18},{18... | collective-permute-start | bytes 4718600 | tf_op jit(solution)/shard_map/ppermute | solution.py:12
  92.5 85.3 %collective-permute-start.1 = (f32[1536,256]{1,0:T(8,128)S(1)}, f32[1536,256]{1,0:T(8,128)S(1)}, u32[]{:S(2)}, u32[]{:S(2)}) collective-permute-start(f32[1536,256]{1,0:T(8,128)S(1)} %bitcast.20), channel_id=1, source_target_pairs={{0,30},{2,0},{4,2},{6,4},{8,6},{10,8},{12,10},{14,12},{16,14},{18,... | collective-permute-start | bytes 4718600 | tf_op jit(solution)/shard_map/ppermute | solution.py:12
  96.9 100.2 %collective-permute-start = (f32[1536,256]{1,0:T(8,128)S(1)}, f32[1536,256]{1,0:T(8,128)S(1)}, u32[]{:S(2)}, u32[]{:S(2)}) collective-permute-start(f32[1536,256]{1,0:T(8,128)S(1)} %bitcast.19), channel_id=1, source_target_pairs={{0,28},{2,30},{4,0},{6,2},{8,4},{10,6},{12,8},{14,10},{16,12},{18,... | collective-permute-start | bytes 4718600 | tf_op jit(solution)/shard_map/ppermute | solution.py:12
  198.8 25.0 %copy-start.2 = (bf16[768,256]{1,0:T(8,128)(2,1)S(1)}, bf16[768,256]{1,0:T(8,128)(2,1)}, u32[]{:S(2)}) copy-start(bf16[768,256]{1,0:T(8,128)(2,1)} %param.9) | copy-start | bytes 1179652
  198.8 157.7 %all-reduce.2.cloned.1.call-start = ((), (), s32[]{:S(2)}) async-start(), calls=%async_computation.2 | async-start | bytes 524288 | tf_op jit(solution)/shard_map/psum | solution.py:34
  223.8 2.3 copy-start.1
Sparse Core Ops, SparseCore 0:
  198.9 24.8 reduce-scatter.1
  229.9 126.5 all-reduce.1
where the time goes:
time: 365 us
  waiting for transfers between devices  254 us (70%)
  other arithmetic  43.5 us (12%)
  local copies, waits for them, and re-layouts  29.9 us (8%)
  matrix products  15.4 us (4%)
  between operations  14.1 us (4%)
  starting transfers between devices  7.82 us (2%)
    psum x1, waiting for transfers between devices, local(): lax.psum(weight_term, ('blk', 'rep')) * (1.0 / math.sqrt(node_count))  129 us
    ppermute x4, waiting for transfers between devices, shifted(): lax.ppermute(value, axis, [(i, (i + by) % devices) for i in range(devices)])  99.9 us
    scatter-add x1, other arithmetic, local(): jax.ops.segment_sum(tiles, block_cols, num_segments=spans * stripe_blocks)  38 us
    reduce_scatter x1, waiting for transfers between devices, local(): mine = lax.psum_scatter(total, 'rep', scatter_dimension=0, tiled=True)  25 us
    dot_general x1, local copies, waits for them, and re-layouts, local(): jnp.einsum('kab,kaf->kbf', block_values, picked, preferred_element_type=j...  15.6 us
    dot_general x1, matrix products, local(): jnp.einsum('kab,kaf->kbf', block_values, picked, preferred_element_type=j...  12.1 us
    ppermute x4, starting transfers between devices, shifted(): lax.ppermute(value, axis, [(i, (i + by) % devices) for i in range(devices)])  7.74 us
  transfers between devices with their start and end apart: 6, of which 4 were waited for; matrix products, arithmetic and copies ran while one was open for 0% of the time, Pallas kernels for 0%

commit v1 on v0

--- a/solution.py
+++ b/solution.py
@@ -31,7 +31,13 @@
     feats = jnp.maximum(prev_pre, jnp.zeros_like(prev_pre))
     weight_term = jnp.dot(feats.T, dy_rows, preferred_element_type=jnp.float32)
     node_count = stripe_rows * lax.axis_size("blk")
-    grad_weight = lax.psum(weight_term, ("blk", "rep")) * (1.0 / math.sqrt(node_count))
+
+    def cube_do(load, dev_axis):
+        then = lax.all_gather(load, axis_name=dev_axis)
+        x_new = jnp.sum(then, 0)
+        return x_new
+
+    grad_weight = cube_do(weight_term, ("blk", "rep")) * (1.0 / math.sqrt(node_count))
     grad_in = (
         jnp.dot(dy_rows, weight.T, preferred_element_type=jnp.float32)
         * (prev_pre > 0).astype(jnp.float32)

time: 365 us -> 316 us (0.87)
  waiting for transfers between devices: 254 us -> 202 us
    psum x1 -> x0, waiting for transfers between devices: 129 us -> none  [local(): lax.psum(weight_term, ('blk', 'rep')) * (1.0 / math.sqrt(node_count))]
    all_gather x0 -> x1, waiting for transfers between devices: none -> 77.4 us  [cube_do(): then = lax.all_gather(load, axis_name=dev_axis)]
    reduce_sum x0 -> x1, other arithmetic: none -> 3.93 us  [cube_do(): x_new = jnp.sum(then, 0)]
where the time goes in v1:
time: 316 us
  waiting for transfers between devices  202 us (64%)
  other arithmetic  46.5 us (15%)
  local copies, waits for them, and re-layouts  29.9 us (9%)
  matrix products  15.4 us (5%)
  between operations  14.1 us (4%)
  starting transfers between devices  7.82 us (2%)
    ppermute x4, waiting for transfers between devices, shifted(): lax.ppermute(value, axis, [(i, (i + by) % devices) for i in range(devices)])  99.9 us
    all_gather x1, waiting for transfers between devices, cube_do(): then = lax.all_gather(load, axis_name=dev_axis)  77.4 us
    scatter-add x1, other arithmetic, local(): jax.ops.segment_sum(tiles, block_cols, num_segments=spans * stripe_blocks)  38 us
    reduce_scatter x1, waiting for transfers between devices, local(): mine = lax.psum_scatter(total, 'rep', scatter_dimension=0, tiled=True)  25 us
    dot_general x1, local copies, waits for them, and re-layouts, local(): jnp.einsum('kab,kaf->kbf', block_values, picked, preferred_element_type=j...  15.6 us
    dot_general x1, matrix products, local(): jnp.einsum('kab,kaf->kbf', block_values, picked, preferred_element_type=j...  12.1 us
    ppermute x4, starting transfers between devices, shifted(): lax.ppermute(value, axis, [(i, (i + by) % devices) for i in range(devices)])  7.74 us
    gather x1, local copies, waits for them, and re-layouts, local(): picked = masked.reshape(stripe_blocks, block_size, width)[block_rows]  6.39 us
  transfers between devices with their start and end apart: 6, of which 4 were waited for; matrix products, arithmetic and copies ran while one was open for 0% of the time, Pallas kernels for 0%

profile of v1, /device:TPU:0, one launch (start us, length us, event | category | flops | bytes accessed | tf_op | source)
XLA Modules:
  0.0 316.0 jit_solution(16442731689333005880)
XLA Ops:
  7.2 0.0 copy-start
  7.2 0.0 reduce-scatter.2.cloned.1.call-start
  7.2 0.7 compare_select_fusion.1
  7.9 1.5 compare_select_fusion
  9.4 6.4 %gather_fusion = bf16[120,128,256]{2,1,0:T(8,128)(2,1)} fusion(bf16[12,128,256]{2,1,0:T(8,128)(2,1)S(1)} %bitcast.19, s32[1024]{0:T(1024)S(1)} %pad_clamp_fusion), kind=kCustom, calls=%fused_computation | custom fusion | bytes 15729120 | tf_op jit(solution)/shard_map/gather | solution.py:21
  15.8 12.1 %convolution_bitcast_fusion = f32[120,128,256]{1,2,0:T(8,128)} fusion(bf16[120,128,256]{2,1,0:T(8,128)(2,1)} %gather_fusion, bf16[120,128,128]{2,1,0:T(8,128)(2,1)} %param.11), kind=kOutput, calls=%fused_computation.2 | convolution fusion | flops 1006632960 | bytes 27525120 | tf_op jit(solution)/shard_map/kab,kaf->kbf/dot_general | solution.py:22
  27.9 15.6 %copy.11 = f32[120,128,256]{2,1,0:T(8,128)} copy(f32[120,128,256]{1,2,0:T(8,128)} %convolution_bitcast_fusion) | data formatting | bytes 31457280 | tf_op jit(solution)/shard_map/kab,kaf->kbf/dot_general | solution.py:22
  43.5 0.0 copy-start.3
  43.5 4.1 %broadcast_in_dim.9 = f32[60,128,256]{2,1,0:T(8,128)} broadcast(f32[]{:T(128)} %constant.6.clone.1), dimensions={} | broadcast | bytes 7864324 | tf_op jit(solution)/shard_map/broadcast_in_dim | solution.py:23
  47.5 0.0 copy-done.3
  47.5 38.0 %scatter_fusion = f32[60,128,256]{2,1,0:T(8,128)} fusion(f32[60,128,256]{2,1,0:T(8,128)} %broadcast_in_dim.9, s32[120]{0:T(128)S(1)} %copy-done.3, f32[120,128,256]{2,1,0:T(8,128)} %copy.11), kind=kCustom, calls=%fused_computation.1 | custom fusion | flops 3932160 | bytes 47186400 | tf_op jit(solution)/shard_map/scatter-add | solution.py:23
  85.6 3.9 %fusion.10 = (f32[12,128,256]{2,1,0:T(8,128)S(1)}, f32[12,128,256]{2,1,0:T(8,128)S(1)}, f32[12,128,256]{2,1,0:T(8,128)S(1)}, f32[12,128,256]{2,1,0:T(8,128)S(1)}, f32[12,128,256]{2,1,0:T(8,128)S(1)}) fusion(f32[60,128,256]{2,1,0:T(8,128)} %scatter_fusion), kind=kLoop, calls=%fused_computation.19 | loop fusion | bytes 15728640 | tf_op jit(solution)/shard_map/slice | solution.py:25
  89.4 3.0 collective-permute-start.3
  92.5 0.0 collective-permute-start.2
  92.5 4.4 %collective-permute-start.1 = (f32[1536,256]{1,0:T(8,128)S(1)}, f32[1536,256]{1,0:T(8,128)S(1)}, u32[]{:S(2)}, u32[]{:S(2)}) collective-permute-start(f32[1536,256]{1,0:T(8,128)S(1)} %bitcast.22), channel_id=1, source_target_pairs={{0,30},{2,0},{4,2},{6,4},{8,6},{10,8},{12,10},{14,12},{16,14},{18,... | collective-permute-start | bytes 4718600 | tf_op jit(solution)/shard_map/ppermute | solution.py:12
  96.9 0.3 collective-permute-start
  97.2 80.6 %collective-permute-done.3 = f32[1536,256]{1,0:T(8,128)S(1)} collective-permute-done((f32[1536,256]{1,0:T(8,128)S(1)}, f32[1536,256]{1,0:T(8,128)S(1)}, u32[]{:S(2)}, u32[]{:S(2)}) %collective-permute-start.3) | collective-permute-done | bytes 1572896 | tf_op jit(solution)/shard_map/ppermute | solution.py:12
  177.8 0.0 collective-permute-done.2
  177.8 0.0 collective-permute-done.1
  177.8 19.3 %collective-permute-done = f32[1536,256]{1,0:T(8,128)S(1)} collective-permute-done((f32[1536,256]{1,0:T(8,128)S(1)}, f32[1536,256]{1,0:T(8,128)S(1)}, u32[]{:S(2)}, u32[]{:S(2)}) %collective-permute-start) | collective-permute-done | bytes 1572896 | tf_op jit(solution)/shard_map/ppermute | solution.py:12
  197.1 1.7 fusion.2
  198.8 0.0 copy-start.2
  198.8 0.0 reduce-scatter.2.cloned.1.call-update
  198.8 0.0 all-gather.3.cloned.1.call-start
  198.9 25.0 %reduce-scatter.2.cloned.1.call-done = f32[768,256]{1,0:T(8,128)} async-done(((f32[1536,256]{1,0:T(8,128)}), f32[768,256]{1,0:T(8,128)}) %reduce-scatter.2.cloned.1.call-update) | async-done | bytes 786448 | tf_op jit(solution)/shard_map/reduce_scatter | solution.py:29
  223.8 0.0 copy-done.2
  223.8 0.0 copy-start.1
  223.8 2.2 fusion.4
  226.0 0.0 all-gather.3.cloned.1.call-update
  226.1 0.0 copy-done
  226.1 0.0 copy-done.1
  226.1 1.1 fusion.3
  227.1 77.4 %all-gather.3.cloned.1.call-done = f32[8192,256]{1,0:T(8,128)} async-done(((f32[256,256]{1,0:T(8,128)}), f32[8192,256]{1,0:T(8,128)}) %all-gather.3.cloned.1.call-update) | async-done | bytes 8388624 | tf_op jit(solution)/shard_map/all_gather | solution.py:36
  304.5 3.9 %reduce_sum.9 = f32[256,256]{1,0:T(8,128)S(1)} reduce(f32[32,256,256]{2,1,0:T(8,128)} %bitcast.20, f32[]{:T(128)} %constant.6.clone.1), dimensions={0}, to_apply=%region_2.0 | reduce | flops 2031616 | bytes 8650756 | tf_op jit(solution)/shard_map/reduce_sum | solution.py:37
  308.4 0.7 broadcast_multiply_fusion
  (1 shorter events, 0.0 us)
Async XLA Ops:
  7.2 218.9 %copy-start = (bf16[256,256]{1,0:T(8,128)(2,1)S(1)}, bf16[256,256]{1,0:T(8,128)(2,1)}, u32[]{:S(2)}) copy-start(bf16[256,256]{1,0:T(8,128)(2,1)} %param.10) | copy-start | bytes 393220
  7.2 216.7 %reduce-scatter.2.cloned.1.call-start = ((), (), s32[]{:S(2)}) async-start(), calls=%async_computation.1 | async-start | bytes 2359296 | tf_op jit(solution)/shard_map/reduce_scatter | solution.py:29
  43.5 4.1 %copy-start.3 = (s32[120]{0:T(128)S(1)}, s32[120]{0:T(128)}, u32[]{:S(2)}) copy-start(s32[120]{0:T(128)} %param.13) | copy-start | bytes 1444
  89.4 88.4 %collective-permute-start.3 = (f32[1536,256]{1,0:T(8,128)S(1)}, f32[1536,256]{1,0:T(8,128)S(1)}, u32[]{:S(2)}, u32[]{:S(2)}) collective-permute-start(f32[1536,256]{1,0:T(8,128)S(1)} %bitcast.24), channel_id=1, source_target_pairs={{0,4},{2,6},{4,8},{6,10},{8,12},{10,14},{12,16},{14,18},{16,20},{1... | collective-permute-start | bytes 4718600 | tf_op jit(solution)/shard_map/ppermute | solution.py:12
  92.5 85.3 %collective-permute-start.2 = (f32[1536,256]{1,0:T(8,128)S(1)}, f32[1536,256]{1,0:T(8,128)S(1)}, u32[]{:S(2)}, u32[]{:S(2)}) collective-permute-start(f32[1536,256]{1,0:T(8,128)S(1)} %bitcast.23), channel_id=1, source_target_pairs={{0,2},{2,4},{4,6},{6,8},{8,10},{10,12},{12,14},{14,16},{16,18},{18... | collective-permute-start | bytes 4718600 | tf_op jit(solution)/shard_map/ppermute | solution.py:12
  92.5 85.3 %collective-permute-start.1 = (f32[1536,256]{1,0:T(8,128)S(1)}, f32[1536,256]{1,0:T(8,128)S(1)}, u32[]{:S(2)}, u32[]{:S(2)}) collective-permute-start(f32[1536,256]{1,0:T(8,128)S(1)} %bitcast.22), channel_id=1, source_target_pairs={{0,30},{2,0},{4,2},{6,4},{8,6},{10,8},{12,10},{14,12},{16,14},{18,... | collective-permute-start | bytes 4718600 | tf_op jit(solution)/shard_map/ppermute | solution.py:12
  96.9 100.2 %collective-permute-start = (f32[1536,256]{1,0:T(8,128)S(1)}, f32[1536,256]{1,0:T(8,128)S(1)}, u32[]{:S(2)}, u32[]{:S(2)}) collective-permute-start(f32[1536,256]{1,0:T(8,128)S(1)} %bitcast.21), channel_id=1, source_target_pairs={{0,28},{2,30},{4,0},{6,2},{8,4},{10,6},{12,8},{14,10},{16,12},{18,... | collective-permute-start | bytes 4718600 | tf_op jit(solution)/shard_map/ppermute | solution.py:12
  198.8 25.0 %copy-start.2 = (bf16[768,256]{1,0:T(8,128)(2,1)S(1)}, bf16[768,256]{1,0:T(8,128)(2,1)}, u32[]{:S(2)}) copy-start(bf16[768,256]{1,0:T(8,128)(2,1)} %param.9) | copy-start | bytes 1179652
  198.8 105.7 %all-gather.3.cloned.1.call-start = ((), (), s32[]{:S(2)}) async-start(), calls=%async_computation.2 | async-start | bytes 8650752 | tf_op jit(solution)/shard_map/all_gather | solution.py:36
  223.8 2.3 copy-start.1
Sparse Core Ops, SparseCore 0:
  198.9 24.8 reduce-scatter.1
  227.4 77.0 all-gather.2
